TPU v7x, 32 devices: a whole 2x2x4 slice. The times are simulated.
32 devices in a mesh: prow: 4 (over y, core), pcol: 8 (over z, x).
Axes of the slice: x: 2, y: 2, z: 4, core: 2. Of those that a mesh axis runs over, the one named last changes fastest.
Arguments:
- right_side: float32 [8, 256, 128], P(None, 'prow'), may hold values from -6 to 6
- lower_prev: float32 [8, 256, 129024], P(None, 'prow', 'pcol'), may hold values from -0.015625 to 0.015625
- solved_prev: float32 [129024, 128], P('pcol'), may hold values from -6 to 6
- lower_window: float32 [8, 256, 2048], P(None, 'prow', 'pcol'), may hold values from -0.1875 to 0.1875
- inverse_diag: float32 [8, 256, 256], P(None, 'prow'), may hold values from -0.25 to 1.4, as said below
Outputs:
- solution: float32 [8, 256, 128], P(None, 'prow')
Inputs may be any that keep to these rules, and one draw needn't show every extreme that they name: `inverse_diag`: each block is lower triangular: zero above its diagonal, with diagonal entries of 0.7 to 1.4.
All inputs are finite; a program needn't handle non-finite values.
Results may differ from a plain program's by a relative error of at most 0.00011.
Values sent between devices are 32-bit elements; how exact they have to be, the bound alone decides.
No kernel may reach another device: no remote copies, remote signals or barrier semaphores. Data moves between devices by JAX's collectives and lax.ppermute only.
A program may use at most 128 MiB of HBM per device.

v0:
```python
import jax
import jax.numpy as jnp
from jax import lax
from jax.sharding import PartitionSpec as P


def local(right_side, lower_prev, solved_prev, lower_window, inverse_diag):
    highest = lax.Precision.HIGHEST
    blocks = right_side.shape[0]
    local_rows = right_side.shape[1]
    columns = right_side.shape[2]
    block_rows = inverse_diag.shape[2]
    row_start = lax.axis_index("prow") * local_rows
    solved = jnp.zeros((blocks * block_rows, columns), jnp.float32)
    pieces = []
    full_inverse = lax.all_gather(inverse_diag, "prow", axis=1, tiled=True)
    full_window = lax.all_gather(lower_window, "pcol", axis=2, tiled=True)
    for row_block in range(blocks):
        window_term = jnp.dot(
            full_window[row_block], solved, precision=highest, preferred_element_type=jnp.float32
        )
        earlier_part = jnp.dot(
            lower_prev[row_block],
            solved_prev,
            precision=highest,
            preferred_element_type=jnp.float32,
        )
        earlier_here = lax.psum(earlier_part, "pcol")
        local_residual = right_side[row_block] - (earlier_here + window_term)
        residual = lax.all_gather(local_residual, "prow", axis=0, tiled=True)
        whole_rows = jnp.dot(
            full_inverse[row_block], residual, precision=highest, preferred_element_type=jnp.float32
        )
        pieces.append(lax.dynamic_slice_in_dim(whole_rows, row_start, local_rows, 0))
        solved = lax.dynamic_update_slice_in_dim(solved, whole_rows, row_block * block_rows, 0)
    return jnp.stack(pieces)


def solution(mesh):
    in_specs = (
        P(None, "prow", None),
        P(None, "prow", "pcol"),
        P("pcol", None),
        P(None, "prow", "pcol"),
        P(None, "prow", None),
    )
    out_specs = P(None, "prow", None)
    return jax.shard_map(local, mesh=mesh, in_specs=in_specs, out_specs=out_specs, check_vma=False)
```

profile of v0, /device:TPU:0, one launch (start us, length us, event | category | flops | bytes accessed | tf_op | source)
XLA Modules:
  0.0 249.5 jit_solution(15784132453054589347)
XLA Ops:
  6.5 0.0 all-gather.3.cloned.1.call-start
  6.5 0.7 all-gather.3.cloned.1.call-update
  7.3 0.0 all-reduce.4.cloned.1.call-start
  7.3 0.0 copy-start
  7.3 10.3 %fusion.4 = f32[64,128]{1,0:T(8,128)} fusion(f32[16128,128]{1,0:T(8,128)} %param.7, f32[8,64,16128]{2,1,0:T(8,128)} %param.6), kind=kOutput, calls=%fused_computation.4 | convolution fusion | flops 1585446912 | bytes 12419072 | tf_op jit(solution)/shard_map/dot_general | solution.py:22
  17.7 0.0 copy-done
  17.7 8.1 %fusion.6 = f32[64,128]{1,0:T(8,128)} fusion(f32[16128,128]{1,0:T(8,128)S(1)} %copy-done, f32[8,64,16128]{2,1,0:T(8,128)} %param.6), kind=kOutput, calls=%fused_computation.6 | convolution fusion | flops 1585446912 | bytes 12419072 | tf_op jit(solution)/shard_map/dot_general | solution.py:22
  25.8 7.9 %fusion.8 = f32[64,128]{1,0:T(8,128)} fusion(f32[16128,128]{1,0:T(8,128)S(1)} %copy-done, f32[8,64,16128]{2,1,0:T(8,128)} %param.6), kind=kOutput, calls=%fused_computation.8 | convolution fusion | flops 1585446912 | bytes 12419072 | tf_op jit(solution)/shard_map/dot_general | solution.py:22
  33.7 8.1 %fusion.10 = f32[64,128]{1,0:T(8,128)} fusion(f32[16128,128]{1,0:T(8,128)S(1)} %copy-done, f32[8,64,16128]{2,1,0:T(8,128)} %param.6), kind=kOutput, calls=%fused_computation.10 | convolution fusion | flops 1585446912 | bytes 12419072 | tf_op jit(solution)/shard_map/dot_general | solution.py:22
  41.8 7.9 %fusion.12 = f32[64,128]{1,0:T(8,128)} fusion(f32[16128,128]{1,0:T(8,128)S(1)} %copy-done, f32[8,64,16128]{2,1,0:T(8,128)} %param.6), kind=kOutput, calls=%fused_computation.12 | convolution fusion | flops 1585446912 | bytes 12419072 | tf_op jit(solution)/shard_map/dot_general | solution.py:22
  49.7 8.4 %fusion.14 = f32[64,128]{1,0:T(8,128)} fusion(f32[16128,128]{1,0:T(8,128)S(1)} %copy-done, f32[8,64,16128]{2,1,0:T(8,128)} %param.6), kind=kOutput, calls=%fused_computation.14 | convolution fusion | flops 1585446912 | bytes 12419072 | tf_op jit(solution)/shard_map/dot_general | solution.py:22
  58.1 7.9 %fusion = f32[64,128]{1,0:T(8,128)} fusion(f32[16128,128]{1,0:T(8,128)S(1)} %copy-done, f32[8,64,16128]{2,1,0:T(8,128)} %param.6), kind=kOutput, calls=%fused_computation | convolution fusion | flops 1585446912 | bytes 12419072 | tf_op jit(solution)/shard_map/dot_general | solution.py:22
  66.1 0.0 copy-start.3
  66.1 8.2 %fusion.2 = f32[64,128]{1,0:T(8,128)} fusion(f32[16128,128]{1,0:T(8,128)S(1)} %copy-done, f32[8,64,16128]{2,1,0:T(8,128)} %param.6), kind=kOutput, calls=%fused_computation.2 | convolution fusion | flops 1585446912 | bytes 12419072 | tf_op jit(solution)/shard_map/dot_general | solution.py:22
  74.2 0.0 all-reduce.4.cloned.1.call-update
  74.2 0.0 all-gather.5.cloned.1.call-start
  74.3 0.7 all-gather.5.cloned.1.call-update
  75.0 12.2 %all-gather.3.cloned.1.call-done = f32[8,64,2048]{2,1,0:T(8,128)} async-done(((f32[8,64,256]{2,1,0:T(8,128)}), f32[8,64,2048]{2,1,0:T(8,128)}) %all-gather.3.cloned.1.call-update) | async-done | bytes 4194320 | tf_op jit(solution)/shard_map/all_gather | solution.py:17
  87.1 1.2 fusion.38
  88.3 73.8 %all-reduce.4.cloned.1.call-done = (f32[64,128]{1,0:T(8,128)}, f32[64,128]{1,0:T(8,128)}, f32[64,128]{1,0:T(8,128)}, f32[64,128]{1,0:T(8,128)}, f32[64,128]{1,0:...) async-done(((f32[64,128]{1,0:T(8,128)}, f32[64,128]{1,0:T(8,128)}, f32[64,128]{1,0:T(8,128)}, f32[64,128]{1,0:T(8,128)}, f32[64,128]{1,0:T(8,128)}, ...) | async-done | bytes 262160 | tf_op jit(solution)/shard_map/psum | solution.py:28
  162.1 0.0 copy-done.3
  162.1 0.8 bitcast_subtract_fusion
  163.0 5.4 %all_gather.31 = f32[256,128]{1,0:T(8,128)S(1)} all-gather(f32[64,128]{1,0:T(8,128)S(1)} %bitcast_subtract_fusion), channel_id=1, replica_groups=mesh['prow'=4,'pcol'=8] {'prow'}, dimensions={0}, use_global_device_ids=true | all-gather | bytes 163840 | tf_op jit(solution)/shard_map/all_gather | solution.py:30
  168.4 17.4 %all-gather.5.cloned.1.call-done = f32[8,256,256]{2,1,0:T(8,128)} async-done(((f32[8,64,256]{2,1,0:T(8,128)}), f32[8,256,256]{2,1,0:T(8,128)}) %all-gather.5.cloned.1.call-update) | async-done | bytes 2097168 | tf_op jit(solution)/shard_map/all_gather | solution.py:16
  185.8 1.5 fusion.47
  187.3 2.1 fusion.25
  189.4 5.4 %all_gather.33 = f32[256,128]{1,0:T(8,128)S(1)} all-gather(f32[64,128]{1,0:T(8,128)S(1)} %fusion.25), channel_id=1, replica_groups=mesh['prow'=4,'pcol'=8] {'prow'}, dimensions={0}, use_global_device_ids=true | all-gather | bytes 163840 | tf_op jit(solution)/shard_map/all_gather | solution.py:30
  194.8 0.1 bitcast_dynamic-update-slice_fusion.13
  194.9 0.1 dynamic_update_slice.21
  195.0 0.0 copy-start.6
  195.0 1.4 bitcast_dynamic-update-slice_fusion.5
  196.4 2.3 fusion.27
  198.7 5.4 %all_gather.34 = f32[256,128]{1,0:T(8,128)S(1)} all-gather(f32[64,128]{1,0:T(8,128)S(1)} %fusion.27), channel_id=1, replica_groups=mesh['prow'=4,'pcol'=8] {'prow'}, dimensions={0}, use_global_device_ids=true | all-gather | bytes 163840 | tf_op jit(solution)/shard_map/all_gather | solution.py:30
  204.1 1.4 bitcast_dynamic-update-slice_fusion.4
  205.5 0.0 copy-done.8
  205.5 0.0 copy-done.1
  205.5 1.2 fusion.29
  206.7 5.6 %all_gather.35 = f32[256,128]{1,0:T(8,128)S(1)} all-gather(f32[64,128]{1,0:T(8,128)S(1)} %fusion.29), channel_id=1, replica_groups=mesh['prow'=4,'pcol'=8] {'prow'}, dimensions={0}, use_global_device_ids=true | all-gather | bytes 163840 | tf_op jit(solution)/shard_map/all_gather | solution.py:30
  212.3 0.0 copy-done.2
  212.3 0.4 bitcast_dynamic-update-slice_fusion.3
  212.7 0.0 copy-done.7
  212.7 1.2 fusion.31
  213.9 5.4 %all_gather.36 = f32[256,128]{1,0:T(8,128)S(1)} all-gather(f32[64,128]{1,0:T(8,128)S(1)} %fusion.31), channel_id=1, replica_groups=mesh['prow'=4,'pcol'=8] {'prow'}, dimensions={0}, use_global_device_ids=true | all-gather | bytes 163840 | tf_op jit(solution)/shard_map/all_gather | solution.py:30
  219.4 0.4 bitcast_dynamic-update-slice_fusion.2
  219.8 0.0 copy-done.6
  219.8 1.2 fusion.33
  221.0 5.4 %all_gather.37 = f32[256,128]{1,0:T(8,128)S(1)} all-gather(f32[64,128]{1,0:T(8,128)S(1)} %fusion.33), channel_id=1, replica_groups=mesh['prow'=4,'pcol'=8] {'prow'}, dimensions={0}, use_global_device_ids=true | all-gather | bytes 163840 | tf_op jit(solution)/shard_map/all_gather | solution.py:30
  226.4 0.4 bitcast_dynamic-update-slice_fusion.1
  226.9 0.0 copy-done.5
  226.9 1.2 fusion.35
  228.1 5.6 %all_gather.38 = f32[256,128]{1,0:T(8,128)S(1)} all-gather(f32[64,128]{1,0:T(8,128)S(1)} %fusion.35), channel_id=1, replica_groups=mesh['prow'=4,'pcol'=8] {'prow'}, dimensions={0}, use_global_device_ids=true | all-gather | bytes 163840 | tf_op jit(solution)/shard_map/all_gather | solution.py:30
  233.7 0.4 bitcast_dynamic-update-slice_fusion
  234.1 0.0 copy-done.4
  234.2 1.2 fusion.37
  235.4 5.4 %all_gather.39 = f32[256,128]{1,0:T(8,128)S(1)} all-gather(f32[64,128]{1,0:T(8,128)S(1)} %fusion.37), channel_id=1, replica_groups=mesh['prow'=4,'pcol'=8] {'prow'}, dimensions={0}, use_global_device_ids=true | all-gather | bytes 163840 | tf_op jit(solution)/shard_map/all_gather | solution.py:30
  240.8 0.1 bitcast_dynamic-update-slice_fusion.12
  240.9 0.1 bitcast_dynamic-update-slice_fusion.11
  241.0 0.1 bitcast_dynamic-update-slice_fusion.10
  241.1 0.1 bitcast_dynamic-update-slice_fusion.9
  241.2 0.1 bitcast_dynamic-update-slice_fusion.8
  241.2 0.1 bitcast_dynamic-update-slice_fusion.7
  241.3 0.4 fusion.40
  241.7 0.1 bitcast_dynamic-update-slice_fusion.6
  241.8 0.9 copy.7
  (6 shorter events, 0.0 us)
Async XLA Ops:
  6.5 80.6 %all-gather.3.cloned.1.call-start = ((), (), s32[]{:S(2)}) async-start(), calls=%async_computation | async-start | bytes 4718592 | tf_op jit(solution)/shard_map/all_gather | solution.py:17
  7.3 154.9 %all-reduce.4.cloned.1.call-start = ((), (), s32[]{:S(2)}) async-start(), calls=%async_computation.2 | async-start | bytes 524288 | tf_op jit(solution)/shard_map/psum | solution.py:28
  7.3 10.4 %copy-start = (f32[16128,128]{1,0:T(8,128)S(1)}, f32[16128,128]{1,0:T(8,128)}, u32[]{:S(2)}) copy-start(f32[16128,128]{1,0:T(8,128)} %param.7) | copy-start | bytes 24772612
  66.1 96.1 %copy-start.3 = (f32[8,64,128]{2,1,0:T(8,128)S(1)}, f32[8,64,128]{2,1,0:T(8,128)}, u32[]{:S(2)}) copy-start(f32[8,64,128]{2,1,0:T(8,128)} %param.5) | copy-start | bytes 786436
  74.2 111.6 %all-gather.5.cloned.1.call-start = ((), (), s32[]{:S(2)}) async-start(), calls=%async_computation.1 | async-start | bytes 2621440 | tf_op jit(solution)/shard_map/all_gather | solution.py:16
  162.1 43.4 %copy-start.8 = (f32[64,128]{1,0:T(8,128)S(1)}, f32[64,128]{1,0:T(8,128)}, u32[]{:S(2)}) copy-start(f32[64,128]{1,0:T(8,128)} %get-tuple-element.8) | copy-start | bytes 98308
  168.4 44.3 %copy-start.7 = (f32[64,128]{1,0:T(8,128)S(1)}, f32[64,128]{1,0:T(8,128)}, u32[]{:S(2)}) copy-start(f32[64,128]{1,0:T(8,128)} %get-tuple-element.9) | copy-start | bytes 98308
  185.8 19.7 %copy-start.1 = (f32[8,64,2048]{2,1,0:T(8,128)S(1)}, f32[8,64,2048]{2,1,0:T(8,128)}, u32[]{:S(2)}) copy-start(f32[8,64,2048]{2,1,0:T(8,128)} %all-gather.3.cloned.1.call-done) | copy-start | bytes 12582916
  185.8 26.5 %copy-start.2 = (f32[8,256,256]{2,1,0:T(8,128)S(1)}, f32[8,256,256]{2,1,0:T(8,128)}, u32[]{:S(2)}) copy-start(f32[8,256,256]{2,1,0:T(8,128)} %all-gather.5.cloned.1.call-done) | copy-start | bytes 6291460
  195.0 24.8 %copy-start.6 = (f32[64,128]{1,0:T(8,128)S(1)}, f32[64,128]{1,0:T(8,128)}, u32[]{:S(2)}) copy-start(f32[64,128]{1,0:T(8,128)} %get-tuple-element.10) | copy-start | bytes 98308
  198.7 28.2 %copy-start.5 = (f32[64,128]{1,0:T(8,128)S(1)}, f32[64,128]{1,0:T(8,128)}, u32[]{:S(2)}) copy-start(f32[64,128]{1,0:T(8,128)} %get-tuple-element.11) | copy-start | bytes 98308
  206.7 27.4 %copy-start.4 = (f32[64,128]{1,0:T(8,128)S(1)}, f32[64,128]{1,0:T(8,128)}, u32[]{:S(2)}) copy-start(f32[64,128]{1,0:T(8,128)} %get-tuple-element.12) | copy-start | bytes 98308
Sparse Core Ops, SparseCore 0:
  9.4 77.7 all-gather.2
  91.4 70.6 all-reduce.3
  163.8 21.9 all-gather.4
where the time goes:
time: 253 us; the launch traced here: 249 us
  waiting for transfers between devices  105 us (42%)
  matrix products  83.6 us (33%)
  blocking collectives  43.7 us (17%)
  between operations  13.6 us (5%)
    psum x1, waiting for transfers between devices, local(): earlier_here = lax.psum(earlier_part, 'pcol')  73.8 us
    dot_general x8, matrix products, local(): jnp.dot(lower_prev[row_block], solved_prev, precision=highest, preferred_...  66.9 us
    all_gather x8, blocking collectives, local(): residual = lax.all_gather(local_residual, 'prow', axis=0, tiled=True)  43.7 us
    all_gather x1, waiting for transfers between devices, local(): full_inverse = lax.all_gather(inverse_diag, 'prow', axis=1, tiled=True)  17.4 us
    all_gather x1, waiting for transfers between devices, local(): full_window = lax.all_gather(lower_window, 'pcol', axis=2, tiled=True)  12.2 us
    dot_general x7, matrix products, local(): jnp.dot(full_window[row_block], solved, precision=highest, preferred_elem...  10.4 us
    dot_general x8, matrix products, local(): jnp.dot(full_inverse[row_block], residual, precision=highest, preferred_e...  6.33 us
  transfers between devices with their start and end apart: 3, of which 3 were waited for; matrix products, arithmetic and copies ran while one was open for 28% of the time, Pallas kernels for 0%

commit v1 on v0

--- a/solution.py
+++ b/solution.py
@@ -2,6 +2,7 @@
 import jax.numpy as jnp
 from jax import lax
 from jax.sharding import PartitionSpec as P
+from jax.lax import axis_index, axis_size, ppermute
 
 
 def local(right_side, lower_prev, solved_prev, lower_window, inverse_diag):
@@ -27,7 +28,18 @@
         )
         earlier_here = lax.psum(earlier_part, "pcol")
         local_residual = right_side[row_block] - (earlier_here + window_term)
-        residual = lax.all_gather(local_residual, "prow", axis=0, tiled=True)
+        n_slots = axis_size("prow")
+        vals = [(j, (j + 1) % n_slots) for j in range(n_slots)]
+        pile = [(j, (j - 1) % n_slots) for j in range(n_slots)]
+        tile_out, arr_next = ([local_residual], [local_residual])
+        for _ in range(n_slots // 2):
+            tile_out.append(ppermute(tile_out[-1], "prow", perm=vals))
+        for _ in range((n_slots - 1) // 2):
+            arr_next.append(ppermute(arr_next[-1], axis_name="prow", perm=pile))
+        mid_arr = jnp.concatenate([*tile_out[::-1], *arr_next[1:]], 0)
+        residual = jnp.roll(
+            mid_arr, (axis_index("prow") - n_slots // 2) * local_residual.shape[0], axis=0
+        )
         whole_rows = jnp.dot(
             full_inverse[row_block], residual, precision=highest, preferred_element_type=jnp.float32
         )

time: 253 us -> 273 us (1.079)
  blocking collectives: 43.7 us -> 0 us
  waiting for transfers between devices: 105 us -> 142 us
  starting transfers between devices: 0.08 us -> 14.7 us
  matrix products: 83.6 us -> 95.3 us
    all_gather x8 -> x0, blocking collectives: 43.7 us -> none  [local(): residual = lax.all_gather(local_residual, 'prow', axis=0, tiled=True)]
    ppermute x0 -> x24, waiting for transfers between devices: none -> 35.2 us  [the longest x16 35.1 us: local(): tile_out.append(ppermute(tile_out[-1], 'prow', perm=vals))]
    ppermute x0 -> x24, starting transfers between devices: none -> 14.6 us  [the longest x8 13.8 us: local(): arr_next.append(ppermute(arr_next[-1], axis_name='prow', perm=pile))]
    dot_general x8, matrix products: 6.33 us -> 13.2 us  [local(): jnp.dot(full_inverse[row_block], residual, precision=highest, preferred_e...]
    dot_general x7, matrix products: 10.4 us -> 15.2 us  [local(): jnp.dot(full_window[row_block], solved, precision=highest, preferred_elem...]
  transfers between devices with their start and end apart: 3 -> 27, of which waited for: 3 -> 20; matrix products, arithmetic and copies ran while one was open for 28% -> 26% of each run, Pallas kernels for 0% -> 0%
where the time goes in v1:
time: 273 us; the launch traced here: 269 us
  waiting for transfers between devices  142 us (52%)
  matrix products  95.3 us (35%)
  starting transfers between devices  14.7 us (5%)
  between operations  13.7 us (5%)
    psum x1, waiting for transfers between devices, local(): earlier_here = lax.psum(earlier_part, 'pcol')  73.8 us
    dot_general x8, matrix products, local(): jnp.dot(lower_prev[row_block], solved_prev, precision=highest, preferred_...  66.9 us
    ppermute x16, waiting for transfers between devices, local(): tile_out.append(ppermute(tile_out[-1], 'prow', perm=vals))  35.1 us
    all_gather x1, waiting for transfers between devices, local(): full_inverse = lax.all_gather(inverse_diag, 'prow', axis=1, tiled=True)  19.5 us
    dot_general x7, matrix products, local(): jnp.dot(full_window[row_block], solved, precision=highest, preferred_elem...  15.2 us
    ppermute x8, starting transfers between devices, local(): arr_next.append(ppermute(arr_next[-1], axis_name='prow', perm=pile))  13.8 us
    dot_general x8, matrix products, local(): jnp.dot(full_inverse[row_block], residual, precision=highest, preferred_e...  13.2 us
    all_gather x1, waiting for transfers between devices, local(): full_window = lax.all_gather(lower_window, 'pcol', axis=2, tiled=True)  12.1 us
  transfers between devices with their start and end apart: 27, of which 20 were waited for; matrix products, arithmetic and copies ran while one was open for 26% of the time, Pallas kernels for 0%

profile of v1, /device:TPU:0, one launch (start us, length us, event | category | flops | bytes accessed | tf_op | source)
XLA Modules:
  0.0 269.3 jit_solution(6868114484970018094)
XLA Ops:
  6.5 0.7 all-gather.3.cloned.1.call-update
  7.3 10.4 %fusion.4 = f32[64,128]{1,0:T(8,128)} fusion(f32[16128,128]{1,0:T(8,128)} %param.9, f32[8,64,16128]{2,1,0:T(8,128)} %param.8), kind=kOutput, calls=%fused_computation.4 | convolution fusion | flops 1585446912 | bytes 12419072 | tf_op jit(solution)/shard_map/dot_general | solution.py:23
  17.7 8.1 %fusion.6 = f32[64,128]{1,0:T(8,128)} fusion(f32[16128,128]{1,0:T(8,128)S(1)} %copy-done, f32[8,64,16128]{2,1,0:T(8,128)} %param.8), kind=kOutput, calls=%fused_computation.6 | convolution fusion | flops 1585446912 | bytes 12419072 | tf_op jit(solution)/shard_map/dot_general | solution.py:23
  25.8 7.9 %fusion.8 = f32[64,128]{1,0:T(8,128)} fusion(f32[16128,128]{1,0:T(8,128)S(1)} %copy-done, f32[8,64,16128]{2,1,0:T(8,128)} %param.8), kind=kOutput, calls=%fused_computation.8 | convolution fusion | flops 1585446912 | bytes 12419072 | tf_op jit(solution)/shard_map/dot_general | solution.py:23
  33.7 8.1 %fusion.10 = f32[64,128]{1,0:T(8,128)} fusion(f32[16128,128]{1,0:T(8,128)S(1)} %copy-done, f32[8,64,16128]{2,1,0:T(8,128)} %param.8), kind=kOutput, calls=%fused_computation.10 | convolution fusion | flops 1585446912 | bytes 12419072 | tf_op jit(solution)/shard_map/dot_general | solution.py:23
  41.8 7.9 %fusion.12 = f32[64,128]{1,0:T(8,128)} fusion(f32[16128,128]{1,0:T(8,128)S(1)} %copy-done, f32[8,64,16128]{2,1,0:T(8,128)} %param.8), kind=kOutput, calls=%fused_computation.12 | convolution fusion | flops 1585446912 | bytes 12419072 | tf_op jit(solution)/shard_map/dot_general | solution.py:23
  49.7 8.4 %fusion.14 = f32[64,128]{1,0:T(8,128)} fusion(f32[16128,128]{1,0:T(8,128)S(1)} %copy-done, f32[8,64,16128]{2,1,0:T(8,128)} %param.8), kind=kOutput, calls=%fused_computation.14 | convolution fusion | flops 1585446912 | bytes 12419072 | tf_op jit(solution)/shard_map/dot_general | solution.py:23
  58.1 7.9 %fusion = f32[64,128]{1,0:T(8,128)} fusion(f32[16128,128]{1,0:T(8,128)S(1)} %copy-done, f32[8,64,16128]{2,1,0:T(8,128)} %param.8), kind=kOutput, calls=%fused_computation | convolution fusion | flops 1585446912 | bytes 12419072 | tf_op jit(solution)/shard_map/dot_general | solution.py:23
  66.1 8.1 %fusion.2 = f32[64,128]{1,0:T(8,128)} fusion(f32[16128,128]{1,0:T(8,128)S(1)} %copy-done, f32[8,64,16128]{2,1,0:T(8,128)} %param.8), kind=kOutput, calls=%fused_computation.2 | convolution fusion | flops 1585446912 | bytes 12419072 | tf_op jit(solution)/shard_map/dot_general | solution.py:23
  74.3 0.7 all-gather.5.cloned.1.call-update
  75.0 12.1 %all-gather.3.cloned.1.call-done = f32[8,64,2048]{2,1,0:T(8,128)} async-done(((f32[8,64,256]{2,1,0:T(8,128)}), f32[8,64,2048]{2,1,0:T(8,128)}) %all-gather.3.cloned.1.call-update) | async-done | bytes 4194320 | tf_op jit(solution)/shard_map/all_gather | solution.py:18
  87.1 1.2 fusion.38
  88.3 73.8 %all-reduce.4.cloned.1.call-done = (f32[64,128]{1,0:T(8,128)}, f32[64,128]{1,0:T(8,128)}, f32[64,128]{1,0:T(8,128)}, f32[64,128]{1,0:T(8,128)}, f32[64,128]{1,0:...) async-done(((f32[64,128]{1,0:T(8,128)}, f32[64,128]{1,0:T(8,128)}, f32[64,128]{1,0:T(8,128)}, f32[64,128]{1,0:T(8,128)}, f32[64,128]{1,0:T(8,128)}, ...) | async-done | bytes 262160 | tf_op jit(solution)/shard_map/psum | solution.py:29
  162.1 0.8 bitcast_subtract_fusion
  163.0 1.7 collective-permute-start.2
  164.7 1.6 collective-permute-done
  166.3 19.5 %all-gather.5.cloned.1.call-done = f32[8,256,256]{2,1,0:T(8,128)} async-done(((f32[8,64,256]{2,1,0:T(8,128)}), f32[8,256,256]{2,1,0:T(8,128)}) %all-gather.5.cloned.1.call-update) | async-done | bytes 2097168 | tf_op jit(solution)/shard_map/all_gather | solution.py:17
  185.8 1.6 fusion.47
  187.4 1.7 fusion.25
  189.1 0.3 collective-permute-start.3
  189.4 1.5 collective-permute-start.5
  190.9 1.6 collective-permute-done.3
  192.5 0.1 dynamic_update_slice.21
  192.6 3.2 %collective-permute-done.4 = f32[64,128]{1,0:T(8,128)S(1)} collective-permute-done((f32[64,128]{1,0:T(8,128)S(1)}, f32[64,128]{1,0:T(8,128)S(1)}, u32[]{:S(2)}, u32[]{:S(2)}) %collective-permute-start.4) | collective-permute-done | bytes 32800 | tf_op jit(solution)/shard_map/ppermute | solution.py:36
  195.8 1.7 bitcast_dynamic-update-slice_fusion.5
  197.5 2.3 fusion.27
  199.8 1.7 collective-permute-start.8
  201.6 1.6 collective-permute-done.6
  203.2 3.3 %collective-permute-done.7 = f32[64,128]{1,0:T(8,128)S(1)} collective-permute-done((f32[64,128]{1,0:T(8,128)S(1)}, f32[64,128]{1,0:T(8,128)S(1)}, u32[]{:S(2)}, u32[]{:S(2)}) %collective-permute-start.7) | collective-permute-done | bytes 32800 | tf_op jit(solution)/shard_map/ppermute | solution.py:36
  206.5 1.7 bitcast_dynamic-update-slice_fusion.4
  208.2 2.2 fusion.29
  210.5 1.7 collective-permute-start.11
  212.2 1.6 collective-permute-done.9
  213.8 3.3 %collective-permute-done.10 = f32[64,128]{1,0:T(8,128)S(1)} collective-permute-done((f32[64,128]{1,0:T(8,128)S(1)}, f32[64,128]{1,0:T(8,128)S(1)}, u32[]{:S(2)}, u32[]{:S(2)}) %collective-permute-start.10) | collective-permute-done | bytes 32800 | tf_op jit(solution)/shard_map/ppermute | solution.py:36
  217.2 1.7 bitcast_dynamic-update-slice_fusion.3
  218.8 2.2 fusion.31
  221.2 1.7 collective-permute-start.14
  222.9 1.6 collective-permute-done.12
  224.5 0.1 bitcast_dynamic-update-slice_fusion.13
  224.6 3.2 %collective-permute-done.13 = f32[64,128]{1,0:T(8,128)S(1)} collective-permute-done((f32[64,128]{1,0:T(8,128)S(1)}, f32[64,128]{1,0:T(8,128)S(1)}, u32[]{:S(2)}, u32[]{:S(2)}) %collective-permute-start.13) | collective-permute-done | bytes 32800 | tf_op jit(solution)/shard_map/ppermute | solution.py:36
  227.8 1.7 bitcast_dynamic-update-slice_fusion.2
  229.5 2.2 fusion.33
  231.8 0.1 bitcast_dynamic-update-slice_fusion.12
  231.9 1.8 collective-permute-start.17
  233.7 1.5 collective-permute-done.15
  235.1 0.2 collective-permute-start.16
  235.3 0.1 bitcast_dynamic-update-slice_fusion.11
  235.4 3.2 %collective-permute-done.16 = f32[64,128]{1,0:T(8,128)S(1)} collective-permute-done((f32[64,128]{1,0:T(8,128)S(1)}, f32[64,128]{1,0:T(8,128)S(1)}, u32[]{:S(2)}, u32[]{:S(2)}) %collective-permute-start.16) | collective-permute-done | bytes 32800 | tf_op jit(solution)/shard_map/ppermute | solution.py:36
  238.7 1.7 bitcast_dynamic-update-slice_fusion.1
  240.3 2.2 fusion.35
  242.6 0.1 bitcast_dynamic-update-slice_fusion.10
  242.7 1.8 collective-permute-start.20
  244.5 1.5 collective-permute-done.18
  246.0 0.1 bitcast_dynamic-update-slice_fusion.9
  246.1 3.2 %collective-permute-done.19 = f32[64,128]{1,0:T(8,128)S(1)} collective-permute-done((f32[64,128]{1,0:T(8,128)S(1)}, f32[64,128]{1,0:T(8,128)S(1)}, u32[]{:S(2)}, u32[]{:S(2)}) %collective-permute-start.19) | collective-permute-done | bytes 32800 | tf_op jit(solution)/shard_map/ppermute | solution.py:36
  249.3 1.7 bitcast_dynamic-update-slice_fusion
  251.0 2.2 fusion.37
  253.3 0.1 bitcast_dynamic-update-slice_fusion.8
  253.4 1.8 collective-permute-start.23
  255.2 1.5 collective-permute-done.21
  256.8 3.2 %collective-permute-done.22 = f32[64,128]{1,0:T(8,128)S(1)} collective-permute-done((f32[64,128]{1,0:T(8,128)S(1)}, f32[64,128]{1,0:T(8,128)S(1)}, u32[]{:S(2)}, u32[]{:S(2)}) %collective-permute-start.22) | collective-permute-done | bytes 32800 | tf_op jit(solution)/shard_map/ppermute | solution.py:36
  260.0 1.6 fusion.40
  261.6 0.1 bitcast_dynamic-update-slice_fusion.6
  261.7 0.9 copy.7
  (42 shorter events, 0.7 us)
Async XLA Ops:
  6.5 80.6 %all-gather.3.cloned.1.call-start = ((), (), s32[]{:S(2)}) async-start(), calls=%async_computation | async-start | bytes 4718592 | tf_op jit(solution)/shard_map/all_gather | solution.py:18
  7.3 154.9 %all-reduce.4.cloned.1.call-start = ((), (), s32[]{:S(2)}) async-start(), calls=%async_computation.2 | async-start | bytes 524288 | tf_op jit(solution)/shard_map/psum | solution.py:29
  7.3 10.4 %copy-start = (f32[16128,128]{1,0:T(8,128)S(1)}, f32[16128,128]{1,0:T(8,128)}, u32[]{:S(2)}) copy-start(f32[16128,128]{1,0:T(8,128)} %param.9) | copy-start | bytes 24772612
  66.1 96.0 %copy-start.1 = (f32[8,64,128]{2,1,0:T(8,128)S(1)}, f32[8,64,128]{2,1,0:T(8,128)}, u32[]{:S(2)}) copy-start(f32[8,64,128]{2,1,0:T(8,128)} %param.7) | copy-start | bytes 786436
  74.3 111.5 %all-gather.5.cloned.1.call-start = ((), (), s32[]{:S(2)}) async-start(), calls=%async_computation.1 | async-start | bytes 2621440 | tf_op jit(solution)/shard_map/all_gather | solution.py:17
  162.1 46.1 %copy-start.6 = (f32[64,128]{1,0:T(8,128)S(1)}, f32[64,128]{1,0:T(8,128)}, u32[]{:S(2)}) copy-start(f32[64,128]{1,0:T(8,128)} %get-tuple-element.9) | copy-start | bytes 98308
  163.0 3.3 %collective-permute-start = (f32[64,128]{1,0:T(8,128)S(1)}, f32[64,128]{1,0:T(8,128)S(1)}, u32[]{:S(2)}, u32[]{:S(2)}) collective-permute-start(f32[64,128]{1,0:T(8,128)S(1)} %bitcast_subtract_fusion), channel_id=1, source_target_pairs={{0,8},{8,16},{16,24},{24,0},{1,9},{9,17},{17,25},{25,1},{2,10},{10... | collective-permute-start | bytes 98312 | tf_op jit(solution)/shard_map/ppermute | solution.py:36
  163.0 22.8 %collective-permute-start.2 = (f32[64,128]{1,0:T(8,128)S(1)}, f32[64,128]{1,0:T(8,128)S(1)}, u32[]{:S(2)}, u32[]{:S(2)}) collective-permute-start(f32[64,128]{1,0:T(8,128)S(1)} %bitcast_subtract_fusion), channel_id=1, source_target_pairs={{0,24},{8,0},{16,8},{24,16},{1,25},{9,1},{17,9},{25,17},{2,26},{10... | collective-permute-start | bytes 98312 | tf_op jit(solution)/shard_map/ppermute | solution.py:38
  166.3 19.5 %collective-permute-start.1 = (f32[64,128]{1,0:T(8,128)S(1)}, f32[64,128]{1,0:T(8,128)S(1)}, u32[]{:S(2)}, u32[]{:S(2)}) collective-permute-start(f32[64,128]{1,0:T(8,128)S(1)} %collective-permute-done), channel_id=1, source_target_pairs={{0,8},{8,16},{16,24},{24,0},{1,9},{9,17},{17,25},{25,1},{2,10},{10... | collective-permute-start | bytes 98312 | tf_op jit(solution)/shard_map/ppermute | solution.py:36
  166.3 52.5 %copy-start.5 = (f32[64,128]{1,0:T(8,128)S(1)}, f32[64,128]{1,0:T(8,128)}, u32[]{:S(2)}) copy-start(f32[64,128]{1,0:T(8,128)} %get-tuple-element.10) | copy-start | bytes 98308
  189.1 3.4 %collective-permute-start.3 = (f32[64,128]{1,0:T(8,128)S(1)}, f32[64,128]{1,0:T(8,128)S(1)}, u32[]{:S(2)}, u32[]{:S(2)}) collective-permute-start(f32[64,128]{1,0:T(8,128)S(1)} %fusion.25), channel_id=1, source_target_pairs={{0,8},{8,16},{16,24},{24,0},{1,9},{9,17},{17,25},{25,1},{2,10},{10... | collective-permute-start | bytes 98312 | tf_op jit(solution)/shard_map/ppermute | solution.py:36
  189.4 3.2 %collective-permute-start.5 = (f32[64,128]{1,0:T(8,128)S(1)}, f32[64,128]{1,0:T(8,128)S(1)}, u32[]{:S(2)}, u32[]{:S(2)}) collective-permute-start(f32[64,128]{1,0:T(8,128)S(1)} %fusion.25), channel_id=1, source_target_pairs={{0,24},{8,0},{16,8},{24,16},{1,25},{9,1},{17,9},{25,17},{2,26},{10... | collective-permute-start | bytes 98312 | tf_op jit(solution)/shard_map/ppermute | solution.py:38
  192.5 3.3 %collective-permute-start.4 = (f32[64,128]{1,0:T(8,128)S(1)}, f32[64,128]{1,0:T(8,128)S(1)}, u32[]{:S(2)}, u32[]{:S(2)}) collective-permute-start(f32[64,128]{1,0:T(8,128)S(1)} %collective-permute-done.3), channel_id=1, source_target_pairs={{0,8},{8,16},{16,24},{24,0},{1,9},{9,17},{17,25},{25,1},{2,10},{10... | collective-permute-start | bytes 98312 | tf_op jit(solution)/shard_map/ppermute | solution.py:36
  192.6 36.9 %copy-start.4 = (f32[64,128]{1,0:T(8,128)S(1)}, f32[64,128]{1,0:T(8,128)}, u32[]{:S(2)}) copy-start(f32[64,128]{1,0:T(8,128)} %get-tuple-element.11) | copy-start | bytes 98308
  199.8 40.6 %copy-start.3 = (f32[64,128]{1,0:T(8,128)S(1)}, f32[64,128]{1,0:T(8,128)}, u32[]{:S(2)}) copy-start(f32[64,128]{1,0:T(8,128)} %get-tuple-element.12) | copy-start | bytes 98308
  199.8 3.4 %collective-permute-start.6 = (f32[64,128]{1,0:T(8,128)S(1)}, f32[64,128]{1,0:T(8,128)S(1)}, u32[]{:S(2)}, u32[]{:S(2)}) collective-permute-start(f32[64,128]{1,0:T(8,128)S(1)} %fusion.27), channel_id=1, source_target_pairs={{0,8},{8,16},{16,24},{24,0},{1,9},{9,17},{17,25},{25,1},{2,10},{10... | collective-permute-start | bytes 98312 | tf_op jit(solution)/shard_map/ppermute | solution.py:36
  199.8 3.3 %collective-permute-start.8 = (f32[64,128]{1,0:T(8,128)S(1)}, f32[64,128]{1,0:T(8,128)S(1)}, u32[]{:S(2)}, u32[]{:S(2)}) collective-permute-start(f32[64,128]{1,0:T(8,128)S(1)} %fusion.27), channel_id=1, source_target_pairs={{0,24},{8,0},{16,8},{24,16},{1,25},{9,1},{17,9},{25,17},{2,26},{10... | collective-permute-start | bytes 98312 | tf_op jit(solution)/shard_map/ppermute | solution.py:38
  203.2 3.3 %collective-permute-start.7 = (f32[64,128]{1,0:T(8,128)S(1)}, f32[64,128]{1,0:T(8,128)S(1)}, u32[]{:S(2)}, u32[]{:S(2)}) collective-permute-start(f32[64,128]{1,0:T(8,128)S(1)} %collective-permute-done.6), channel_id=1, source_target_pairs={{0,8},{8,16},{16,24},{24,0},{1,9},{9,17},{17,25},{25,1},{2,10},{10... | collective-permute-start | bytes 98312 | tf_op jit(solution)/shard_map/ppermute | solution.py:36
  210.4 3.4 %collective-permute-start.9 = (f32[64,128]{1,0:T(8,128)S(1)}, f32[64,128]{1,0:T(8,128)S(1)}, u32[]{:S(2)}, u32[]{:S(2)}) collective-permute-start(f32[64,128]{1,0:T(8,128)S(1)} %fusion.29), channel_id=1, source_target_pairs={{0,8},{8,16},{16,24},{24,0},{1,9},{9,17},{17,25},{25,1},{2,10},{10... | collective-permute-start | bytes 98312 | tf_op jit(solution)/shard_map/ppermute | solution.py:36
  210.5 3.3 %collective-permute-start.11 = (f32[64,128]{1,0:T(8,128)S(1)}, f32[64,128]{1,0:T(8,128)S(1)}, u32[]{:S(2)}, u32[]{:S(2)}) collective-permute-start(f32[64,128]{1,0:T(8,128)S(1)} %fusion.29), channel_id=1, source_target_pairs={{0,24},{8,0},{16,8},{24,16},{1,25},{9,1},{17,9},{25,17},{2,26},{10... | collective-permute-start | bytes 98312 | tf_op jit(solution)/shard_map/ppermute | solution.py:38
  213.8 3.3 %collective-permute-start.10 = (f32[64,128]{1,0:T(8,128)S(1)}, f32[64,128]{1,0:T(8,128)S(1)}, u32[]{:S(2)}, u32[]{:S(2)}) collective-permute-start(f32[64,128]{1,0:T(8,128)S(1)} %collective-permute-done.9), channel_id=1, source_target_pairs={{0,8},{8,16},{16,24},{24,0},{1,9},{9,17},{17,25},{25,1},{2,10},{10... | collective-permute-start | bytes 98312 | tf_op jit(solution)/shard_map/ppermute | solution.py:36
  218.8 32.2 %copy-start.2 = (f32[64,128]{1,0:T(8,128)S(1)}, f32[64,128]{1,0:T(8,128)}, u32[]{:S(2)}) copy-start(f32[64,128]{1,0:T(8,128)} %get-tuple-element.13) | copy-start | bytes 98308
  221.1 3.4 %collective-permute-start.12 = (f32[64,128]{1,0:T(8,128)S(1)}, f32[64,128]{1,0:T(8,128)S(1)}, u32[]{:S(2)}, u32[]{:S(2)}) collective-permute-start(f32[64,128]{1,0:T(8,128)S(1)} %fusion.31), channel_id=1, source_target_pairs={{0,8},{8,16},{16,24},{24,0},{1,9},{9,17},{17,25},{25,1},{2,10},{10... | collective-permute-start | bytes 98312 | tf_op jit(solution)/shard_map/ppermute | solution.py:36
  221.2 3.4 %collective-permute-start.14 = (f32[64,128]{1,0:T(8,128)S(1)}, f32[64,128]{1,0:T(8,128)S(1)}, u32[]{:S(2)}, u32[]{:S(2)}) collective-permute-start(f32[64,128]{1,0:T(8,128)S(1)} %fusion.31), channel_id=1, source_target_pairs={{0,24},{8,0},{16,8},{24,16},{1,25},{9,1},{17,9},{25,17},{2,26},{10... | collective-permute-start | bytes 98312 | tf_op jit(solution)/shard_map/ppermute | solution.py:38
  224.5 3.3 %collective-permute-start.13 = (f32[64,128]{1,0:T(8,128)S(1)}, f32[64,128]{1,0:T(8,128)S(1)}, u32[]{:S(2)}, u32[]{:S(2)}) collective-permute-start(f32[64,128]{1,0:T(8,128)S(1)} %collective-permute-done.12), channel_id=1, source_target_pairs={{0,8},{8,16},{16,24},{24,0},{1,9},{9,17},{17,25},{25,1},{2,10},{10... | collective-permute-start | bytes 98312 | tf_op jit(solution)/shard_map/ppermute | solution.py:36
  231.7 3.4 %collective-permute-start.15 = (f32[64,128]{1,0:T(8,128)S(1)}, f32[64,128]{1,0:T(8,128)S(1)}, u32[]{:S(2)}, u32[]{:S(2)}) collective-permute-start(f32[64,128]{1,0:T(8,128)S(1)} %fusion.33), channel_id=1, source_target_pairs={{0,8},{8,16},{16,24},{24,0},{1,9},{9,17},{17,25},{25,1},{2,10},{10... | collective-permute-start | bytes 98312 | tf_op jit(solution)/shard_map/ppermute | solution.py:36
  231.9 3.5 %collective-permute-start.17 = (f32[64,128]{1,0:T(8,128)S(1)}, f32[64,128]{1,0:T(8,128)S(1)}, u32[]{:S(2)}, u32[]{:S(2)}) collective-permute-start(f32[64,128]{1,0:T(8,128)S(1)} %fusion.33), channel_id=1, source_target_pairs={{0,24},{8,0},{16,8},{24,16},{1,25},{9,1},{17,9},{25,17},{2,26},{10... | collective-permute-start | bytes 98312 | tf_op jit(solution)/shard_map/ppermute | solution.py:38
  235.1 3.5 %collective-permute-start.16 = (f32[64,128]{1,0:T(8,128)S(1)}, f32[64,128]{1,0:T(8,128)S(1)}, u32[]{:S(2)}, u32[]{:S(2)}) collective-permute-start(f32[64,128]{1,0:T(8,128)S(1)} %collective-permute-done.15), channel_id=1, source_target_pairs={{0,8},{8,16},{16,24},{24,0},{1,9},{9,17},{17,25},{25,1},{2,10},{10... | collective-permute-start | bytes 98312 | tf_op jit(solution)/shard_map/ppermute | solution.py:36
  242.6 3.4 %collective-permute-start.18 = (f32[64,128]{1,0:T(8,128)S(1)}, f32[64,128]{1,0:T(8,128)S(1)}, u32[]{:S(2)}, u32[]{:S(2)}) collective-permute-start(f32[64,128]{1,0:T(8,128)S(1)} %fusion.35), channel_id=1, source_target_pairs={{0,8},{8,16},{16,24},{24,0},{1,9},{9,17},{17,25},{25,1},{2,10},{10... | collective-permute-start | bytes 98312 | tf_op jit(solution)/shard_map/ppermute | solution.py:36
  242.7 3.4 %collective-permute-start.20 = (f32[64,128]{1,0:T(8,128)S(1)}, f32[64,128]{1,0:T(8,128)S(1)}, u32[]{:S(2)}, u32[]{:S(2)}) collective-permute-start(f32[64,128]{1,0:T(8,128)S(1)} %fusion.35), channel_id=1, source_target_pairs={{0,24},{8,0},{16,8},{24,16},{1,25},{9,1},{17,9},{25,17},{2,26},{10... | collective-permute-start | bytes 98312 | tf_op jit(solution)/shard_map/ppermute | solution.py:38
  246.0 3.3 %collective-permute-start.19 = (f32[64,128]{1,0:T(8,128)S(1)}, f32[64,128]{1,0:T(8,128)S(1)}, u32[]{:S(2)}, u32[]{:S(2)}) collective-permute-start(f32[64,128]{1,0:T(8,128)S(1)} %collective-permute-done.18), channel_id=1, source_target_pairs={{0,8},{8,16},{16,24},{24,0},{1,9},{9,17},{17,25},{25,1},{2,10},{10... | collective-permute-start | bytes 98312 | tf_op jit(solution)/shard_map/ppermute | solution.py:36
  253.2 3.4 %collective-permute-start.21 = (f32[64,128]{1,0:T(8,128)S(1)}, f32[64,128]{1,0:T(8,128)S(1)}, u32[]{:S(2)}, u32[]{:S(2)}) collective-permute-start(f32[64,128]{1,0:T(8,128)S(1)} %fusion.37), channel_id=1, source_target_pairs={{0,8},{8,16},{16,24},{24,0},{1,9},{9,17},{17,25},{25,1},{2,10},{10... | collective-permute-start | bytes 98312 | tf_op jit(solution)/shard_map/ppermute | solution.py:36
  253.4 3.4 %collective-permute-start.23 = (f32[64,128]{1,0:T(8,128)S(1)}, f32[64,128]{1,0:T(8,128)S(1)}, u32[]{:S(2)}, u32[]{:S(2)}) collective-permute-start(f32[64,128]{1,0:T(8,128)S(1)} %fusion.37), channel_id=1, source_target_pairs={{0,24},{8,0},{16,8},{24,16},{1,25},{9,1},{17,9},{25,17},{2,26},{10... | collective-permute-start | bytes 98312 | tf_op jit(solution)/shard_map/ppermute | solution.py:38
  256.6 3.3 %collective-permute-start.22 = (f32[64,128]{1,0:T(8,128)S(1)}, f32[64,128]{1,0:T(8,128)S(1)}, u32[]{:S(2)}, u32[]{:S(2)}) collective-permute-start(f32[64,128]{1,0:T(8,128)S(1)} %collective-permute-done.21), channel_id=1, source_target_pairs={{0,8},{8,16},{16,24},{24,0},{1,9},{9,17},{17,25},{25,1},{2,10},{10... | collective-permute-start | bytes 98312 | tf_op jit(solution)/shard_map/ppermute | solution.py:36
Sparse Core Ops, SparseCore 0:
  9.4 77.7 all-gather.2
  91.4 70.6 all-reduce.3
  163.8 21.9 all-gather.4
